TPU v7x, 512 devices: a whole 4x4x16 slice. The times are simulated.
512 devices in a mesh: row: 16 (over y_lo, x, core), col: 32 (over z, y_hi).
Axes of the slice: x: 4, y: 4 (y_hi: 2, y_lo: 2; y = y_hi * 2 + y_lo), z: 16, core: 2. Of those that a mesh axis runs over, the one named last changes fastest.
Arguments:
- coefficients: float32 [8, 8192, 8192], P(None, 'row', 'col'), may hold values from -40 to 40, as said below
- lambdas: float32 [256], replicated, may hold values from -0.95 to 0.95
- right_vecs: float32 [8192, 256], P(('col', 'row')), may hold values from -6 to 6
- left_vecs: float32 [8192, 256], P(('row', 'col')), may hold values from -6 to 6
Outputs:
- right_resid: float32 [8192, 256], P(('row', 'col'))
- left_resid: float32 [8192, 256], P(('col', 'row'))
- root_mean: float32 [2, 256], replicated
Inputs may be any that keep to these rules, and one draw needn't show every extreme that they name: `coefficients`: the entries of every coefficient matrix.
All inputs are finite; a program needn't handle non-finite values.
Results may differ from a plain program's by a relative error of at most 0.0001.
Values sent between devices are 32-bit elements; how exact they have to be, the bound alone decides.
A program may use at most 64 MiB of HBM per device.

v0:
```python
import jax
import jax.numpy as jnp
from jax import lax
from jax.sharding import PartitionSpec as P

N = 8192


epsilon = 1e-06


def chebyshev(lambdas, count):
    terms = [jnp.ones_like(lambdas), lambdas]
    while len(terms) < count:
        terms.append(2.0 * lambdas * terms[-1] - terms[-2])
    return jnp.stack(terms[:count])


def right_term(matrices, weighted):
    total = jnp.dot(
        matrices[0],
        weighted[0],
        precision=lax.Precision.HIGHEST,
        preferred_element_type=jnp.float32,
    )
    for term in range(1, matrices.shape[0]):
        total = total + jnp.dot(
            matrices[term],
            weighted[term],
            precision=lax.Precision.HIGHEST,
            preferred_element_type=jnp.float32,
        )
    return total


def left_term(matrices, weighted):
    numbers = (((0,), (0,)), ((), ()))
    total = lax.dot_general(
        matrices[0],
        weighted[0],
        numbers,
        precision=lax.Precision.HIGHEST,
        preferred_element_type=jnp.float32,
    )
    for term in range(1, matrices.shape[0]):
        total = total + lax.dot_general(
            matrices[term],
            weighted[term],
            numbers,
            precision=lax.Precision.HIGHEST,
            preferred_element_type=jnp.float32,
        )
    return total


def body(coefficients, lambdas, right_vecs, left_vecs):
    weights = chebyshev(lambdas, coefficients.shape[0])
    right_cols = lax.all_gather(right_vecs, "row", axis=0, tiled=True)
    left_rows = lax.all_gather(left_vecs, "col", axis=0, tiled=True)
    right_weighted = right_cols[None, :, :] * weights[:, None, :]
    left_weighted = left_rows[None, :, :] * weights[:, None, :]
    matrices = coefficients
    right_resid = lax.psum_scatter(
        right_term(matrices, right_weighted), "col", scatter_dimension=0, tiled=True
    )
    matrices = coefficients
    left_resid = lax.psum_scatter(
        left_term(matrices, left_weighted), "row", scatter_dimension=0, tiled=True
    )
    right_squares, left_squares = lax.psum(
        (jnp.sum(right_resid * right_resid, axis=0), jnp.sum(left_resid * left_resid, axis=0)),
        ("row", "col"),
    )
    root_mean = jnp.sqrt(jnp.stack([right_squares, left_squares]) / N + epsilon)
    return (right_resid, left_resid, root_mean)


def solution(mesh):
    return jax.shard_map(
        body,
        mesh=mesh,
        in_specs=(P(None, "row", "col"), P(), P(("col", "row"), None), P(("row", "col"), None)),
        out_specs=(P(("row", "col"), None), P(("col", "row"), None), P()),
        check_vma=False,
    )
```

profile of v0, /device:TPU:1, one launch (start us, length us, event | category | flops | bytes accessed | tf_op | source)
XLA Modules:
  0.0 924.4 jit_solution(9988181470796313399)
XLA Ops:
  7.2 0.0 reduce-scatter.9.cloned.1.call-start
  7.2 0.7 multiply_subtract_fusion
  7.9 0.7 multiply_subtract_fusion.1
  8.6 72.7 %all_gather.7 = f32[512,256]{1,0:T(8,128)S(1)} all-gather(f32[16,256]{1,0:T(8,128)} %param.7), channel_id=1, replica_groups=mesh['row'=16,'col'=32] {'col'}, dimensions={0}, use_global_device_ids=true | all-gather | bytes 540672 | tf_op jit(solution)/shard_map/all_gather | solution.py:59
  81.3 0.7 stack.40
  82.0 0.0 copy-start
  82.0 0.4 broadcast_multiply_fusion
  82.4 1.8 copy-done
  84.2 1.0 fusion.2
  85.3 1.0 convolution_add_fusion.13
  86.3 1.0 convolution_add_fusion.12
  87.3 0.0 copy-start.2
  87.3 1.0 convolution_add_fusion.11
  88.4 1.0 convolution_add_fusion.10
  89.4 1.0 convolution_add_fusion.9
  90.4 1.0 convolution_add_fusion.8
  91.5 1.0 fusion.1
  92.5 0.8 copy.13
  93.4 0.0 reduce-scatter.9.cloned.1.call-update
  93.4 0.0 reduce-scatter.7.cloned.1.call-start
  93.4 0.0 copy-done.2
  93.4 0.0 copy-start.1
  93.5 34.1 %all_gather.6 = f32[256,256]{1,0:T(8,128)S(1)} all-gather(f32[16,256]{1,0:T(8,128)S(1)} %copy-done.2), channel_id=1, replica_groups=mesh['row'=16,'col'=32] {'row'}, dimensions={0}, use_global_device_ids=true | all-gather | bytes 278528 | tf_op jit(solution)/shard_map/all_gather | solution.py:58
  127.5 0.2 broadcast_multiply_fusion.1
  127.7 2.1 fusion.18
  129.8 2.1 convolution_add_fusion.6
  131.9 0.0 copy-done.1
  131.9 1.0 convolution_add_fusion.5
  133.0 1.0 convolution_add_fusion.4
  134.0 1.0 convolution_add_fusion.3
  135.1 1.0 convolution_add_fusion.2
  136.1 1.0 convolution_add_fusion.1
  137.2 1.0 fusion
  138.2 1.0 copy.11
  139.2 0.0 reduce-scatter.7.cloned.1.call-update
  139.2 27.8 %reduce-scatter.9.cloned.1.call-done = f32[16,256]{1,0:T(8,128)} async-done(((f32[256,256]{1,0:T(8,128)}), f32[16,256]{1,0:T(8,128)}) %reduce-scatter.9.cloned.1.call-update) | async-done | bytes 16400
  167.0 0.8 copy.14
  167.9 0.1 multiply_reduce_fusion
  168.0 635.2 %reduce-scatter.7.cloned.1.call-done = f32[16,256]{1,0:T(8,128)} async-done(((f32[512,256]{1,0:T(8,128)}), f32[16,256]{1,0:T(8,128)}) %reduce-scatter.7.cloned.1.call-update) | async-done | bytes 16400
  803.2 0.8 copy.12
  804.0 0.1 multiply_reduce_fusion.1
  804.1 112.8 %all-reduce = (f32[1,256]{1,0:T(1,128)S(1)}, f32[1,256]{1,0:T(1,128)S(1)}) all-reduce(f32[1,256]{1,0:T(1,128)S(1)} %bitcast.105, f32[1,256]{1,0:T(1,128)S(1)} %bitcast.106), channel_id=1, replica_groups=mesh['row'=16,'col'=32] {'row','col'}, use_global_device_ids=true, to_apply=%region_5.0 | all-reduce | flops 512 | bytes 4096 | tf_op jit(solution)/shard_map/psum | solution.py:70
  916.9 0.6 fusion.37
  (1 shorter events, 0.0 us)
Async XLA Ops:
  7.2 159.9 %reduce-scatter.9.cloned.1.call-start = ((), (), s32[]{:S(2)}) async-start(), calls=%async_computation.3 | async-start | bytes 278528
  82.0 2.2 copy-start
  87.3 6.1 copy-start.2
  93.4 709.8 %reduce-scatter.7.cloned.1.call-start = ((), (), s32[]{:S(2)}) async-start(), calls=%async_computation.2 | async-start | bytes 540672
  93.4 38.5 %copy-start.1 = (f32[8,512,256]{2,1,0:T(8,128)S(1)}, f32[8,512,256]{2,1,0:T(8,128)}, u32[]{:S(2)}) copy-start(f32[8,512,256]{2,1,0:T(8,128)} %param.4) | copy-start | bytes 12582916
Sparse Core Ops, SparseCore 0:
  93.5 73.4 reduce-scatter.8
  172.0 631.1 reduce-scatter.6
where the time goes:
time: 925 us; the launch traced here: 924 us
  waiting for transfers between devices  663 us (72%)
  blocking collectives  220 us (24%)
  matrix products  18.7 us (2%)
  between operations  14.2 us (2%)
    unnamed x4, waiting for transfers between devices  663 us
    psum x1, blocking collectives, body(): lax.psum((jnp.sum(right_resid * right_resid, axis=0), jnp.sum(left_resid...  113 us
    all_gather x1, blocking collectives, body(): left_rows = lax.all_gather(left_vecs, 'col', axis=0, tiled=True)  72.7 us
    all_gather x1, blocking collectives, body(): right_cols = lax.all_gather(right_vecs, 'row', axis=0, tiled=True)  34.1 us
  transfers between devices with their start and end apart: 2, of which 2 were waited for; matrix products, arithmetic and copies ran while one was open for 1% of the time, Pallas kernels for 0%

commit v1 on v0

v1 whole, which is shorter than its diff:
```python
import functools

import jax
import jax.numpy as jnp
from jax import lax
from jax.experimental import pallas as pl
from jax.experimental.pallas import tpu as pltpu
from jax.sharding import PartitionSpec as P

MESH = pl.DeviceIdType.MESH
N = 8192
K = 8
TRIP = 256
NX, NY, NZ = 4, 4, 16
EPSILON = 1e-06
F32 = jnp.float32
BF16 = jnp.bfloat16

ROW_OFFSETS = [(dx, dy, dc) for dx in (2, 1, 3, 0) for dy in (1, 0) for dc in (0, 1) if dx or dy or dc]
PLANE_OFFSETS = [(dx, dy, dc) for dx in (2, 1, 3, 0) for dy in (2, 1, 3, 0) for dc in (0, 1) if dx or dy or dc]
Z_OFFSETS = [8, 7, 9, 6, 10, 5, 11, 4, 12, 3, 13, 2, 14, 1, 15]


def split(value):
    high = value.astype(BF16)
    low = (value - high.astype(F32)).astype(BF16)
    return high, low


def dot(a, b):
    return jnp.dot(a, b, preferred_element_type=F32)


def kernel(
    a_hbm, lam_hbm, x_hbm, y_hbm, right_hbm, left_hbm, mean_ref,
    a_buf, a_hi, a_lo, lam_buf, w_row, w_col, x_buf, y_buf, y_t, r_acc, l_acc, l_out,
    relay_in, relay_out, raw_in, half_in, l_in, fin_r, fin_l, plane_buf, z_buf,
    a_sem, loc_sem, send_sem, x_sem, y_sem, yr_sem, yd_sem, rr_sem, raw_sem, half_sem, l_sem, p_sem, z_sem,
):
    row, col = lax.axis_index("row"), lax.axis_index("col")
    y_lo, x, core = row // 8, (row // 2) % 4, row % 2
    z, y_hi = col // 2, col % 2

    def row_at(off):
        dx, dy, dc = off
        return ((y_lo + dy) % 2) * 8 + ((x + dx) % 4) * 2 + (core + dc) % 2

    def row_dev(off):
        return (row_at(off), col)

    def plane_dev(off):
        dx, dy, dc = off
        yy = (y_hi * 2 + y_lo + dy) % 4
        return ((yy % 2) * 8 + ((x + dx) % 4) * 2 + (core + dc) % 2, z * 2 + yy // 2)

    def z_dev(dz):
        return (row, ((z + dz + 16) % 16) * 2 + y_hi)

    y_dev = (row, z * 2 + (1 - y_hi))

    def remote(src, dst, ssem, rsem, dev):
        return pltpu.make_async_remote_copy(
            src_ref=src, dst_ref=dst, send_sem=ssem, recv_sem=rsem, device_id=dev, device_id_type=MESH
        )

    for j in range(NZ):
        rows = pl.multiple_of(((z + j) % 16) * 32, 32)
        pltpu.make_async_copy(
            a_hbm.at[:, pl.ds(rows, 32), :], a_buf.at[:, pl.ds(j * 32, 32), :], a_sem.at[j]
        ).start()
    my_x = pl.multiple_of(row * 16, 16)
    mine, other = pl.multiple_of(y_hi * 16, 16), pl.multiple_of((1 - y_hi) * 16, 16)
    local = [
        pltpu.make_async_copy(lam_hbm, lam_buf, loc_sem.at[0]),
        pltpu.make_async_copy(x_hbm, x_buf.at[pl.ds(my_x, 16), :], loc_sem.at[1]),
        pltpu.make_async_copy(y_hbm, y_buf.at[0, pl.ds(mine, 16), :], loc_sem.at[2]),
    ]
    for copy in local:
        copy.start()

    barrier = pltpu.get_barrier_semaphore()
    partners = [row_dev(off) for off in ROW_OFFSETS] + [z_dev(1), z_dev(-1), z_dev(2), z_dev(-2), y_dev]
    for dev in partners:
        pl.semaphore_signal(barrier, inc=1, device_id=dev, device_id_type=MESH)
    pl.semaphore_wait(barrier, len(partners))

    def y_slot(rel, chunk):
        return y_buf.at[rel % 16, pl.ds(mine if chunk == 0 else other, 16), :]

    def y_forward(rel, chunk, up, src=None):
        src = y_slot(rel, chunk) if src is None else src
        step = abs(rel) // 2
        sign = 1 if up else -1
        if up or step < 3:
            remote(
                src, y_slot(rel - 2 * sign, chunk), send_sem.at[1], yr_sem.at[chunk, 0 if up else 1, step], z_dev(2 * sign)
            ).start()
        remote(src, y_slot(rel - sign, chunk), send_sem.at[1], yd_sem.at[chunk, 0 if up else 1, step], z_dev(sign)).start()

    def y_wait_relay(rel, chunk, up):
        sem = yr_sem.at[chunk, 0 if up else 1, abs(rel) // 2 - 1]
        remote(y_slot(rel, chunk), y_slot(rel, chunk), send_sem.at[1], sem, y_dev).wait_recv()

    def y_service(step, chunk):
        for up in (True, False):
            rel = -2 * step if up else 2 * step
            y_wait_relay(rel, chunk, up)
            y_forward(rel, chunk, up)

    for up in (True, False):
        y_forward(0, 0, up, src=y_hbm)
    remote(y_hbm, y_slot(0, 0), send_sem.at[1], y_sem, y_dev).start()
    for off in ROW_OFFSETS:
        remote(x_hbm, x_buf.at[pl.ds(my_x, 16), :], send_sem.at[0], x_sem, row_dev(off)).start()

    local[0].wait()
    lam = lam_buf[...]
    terms = [jnp.ones_like(lam), lam]
    while len(terms) < K:
        terms.append(2.0 * lam * terms[-1] - terms[-2])
    for k in range(K):
        w_row[k] = terms[k]
    lam_col = jnp.transpose(jnp.broadcast_to(lam, (128, TRIP)))
    w_col[0] = jnp.ones_like(lam_col)
    w_col[1] = lam_col
    for k in range(2, K):
        w_col[k] = 2.0 * lam_col * w_col[k - 1] - w_col[k - 2]

    def convert(j):
        rows = pl.ds(pl.multiple_of(j * 32, 32), 32)
        pltpu.make_async_copy(a_hbm.at[:, pl.ds(0, 32), :], a_buf.at[:, rows, :], a_sem.at[j]).wait()
        for k in range(K):
            a_hi[k, rows, :], a_lo[k, rows, :] = split(a_buf[k, rows, :])

    def convert_some(start, stop):
        @pl.loop(start, stop)
        def _(j):
            convert(j)

    def y_partner():
        remote(y_slot(0, 1), y_slot(0, 1), send_sem.at[1], y_sem, y_dev).wait_recv()
        for up in (True, False):
            y_forward(0, 1, up)

    convert_some(0, 8)
    y_partner()
    convert_some(8, 16)
    y_service(1, 0)

    local[1].wait()
    remote(x_buf.at[pl.ds(0, 240), :], x_buf.at[pl.ds(0, 240), :], send_sem.at[0], x_sem, y_dev).wait_recv()

    def right_term(k, first):
        xh, xl = split(x_buf[...] * w_row[k])
        ah, al = a_hi[k], a_lo[k]
        part = dot(ah, xh) + dot(al, xh) + dot(ah, xl)
        if first:
            r_acc[...] = part
        else:
            r_acc[...] += part

    def right_some(start, stop):
        @pl.loop(start, stop)
        def _(k):
            right_term(k, False)

    right_term(0, True)
    y_service(1, 1)
    right_some(1, 3)
    y_service(2, 0)
    right_some(3, 8)

    def r_rows(rel, half=None):
        if half is None:
            return pl.ds((rel % 16) * 32, 32)
        return pl.ds((rel % 16) * 32 + half * 16, 16)

    def relay(rel, half, up, src):
        i = (8 - rel) // 2 if up else (rel + 6) // 2
        d = 0 if up else 1
        return remote(
            src, relay_in.at[d, i, pl.ds(half * 16, 16), :], send_sem.at[2], rr_sem.at[d, i, half], z_dev(2 if up else -2)
        )

    for half in (0, 1):
        relay(8, half, True, r_acc.at[r_rows(8, half), :]).start()
    for i in range(4):
        for up in (True, False):
            rel, d = (7 - 2 * i, 0) if up else (2 * i - 7, 1)
            remote(
                r_acc.at[r_rows(rel), :], raw_in.at[d, i], send_sem.at[3], raw_sem.at[d, i], z_dev(1 if up else -1)
            ).start()

    def raw_wait(i, d):
        remote(raw_in.at[d, i], raw_in.at[d, i], send_sem.at[3], raw_sem.at[d, i], y_dev).wait_recv()

    def relay_wait(d, i, half):
        ref = relay_in.at[d, i, pl.ds(half * 16, 16), :]
        remote(ref, ref, send_sem.at[2], rr_sem.at[d, i, half], y_dev).wait_recv()

    def r_service(step):
        for d, up in ((1, False), (0, True)):
            raw_wait(step, d)
            rel = 6 - 2 * step if up else 2 * step - 6
            for half in (0, 1):
                hs = pl.ds(half * 16, 16)
                total = r_acc[r_rows(rel, half), :] + raw_in[d, step, hs, :]
                if up or step > 0:
                    i = step if up else step - 1
                    relay_wait(d, i, half)
                    total = total + relay_in[d, i, hs, :]
                relay_out[d, step, hs, :] = total
                relay(rel, half, up, relay_out.at[d, step, hs, :]).start()

    y_service(2, 1)
    y_service(3, 0)
    r_service(0)
    def y_service3(chunk):
        for up in (True, False):
            rel = -6 if up else 6
            y_wait_relay(rel, chunk, up)
            y_forward(rel, chunk, up)

    y_service3(1)

    def y_finish():
        for chunk in (0, 1):
            y_wait_relay(-8, chunk, True)
            for d in (0, 1):
                for step in range(4):
                    rel = -(2 * step + 1) if d == 0 else 2 * step + 1
                    remote(y_slot(rel, chunk), y_slot(rel, chunk), send_sem.at[1], yd_sem.at[chunk, d, step], y_dev).wait_recv()
        local[2].wait()

    y_finish()
    for j in range(4):
        y_t[:, j * 128 : (j + 1) * 128] = jnp.transpose(
            jnp.concatenate([y_buf[4 * j + i] for i in range(4)], axis=0)
        )

    def left_term(k, first):
        w = w_col[k]
        yh, yl = split(y_t[...] * jnp.concatenate([w] * 4, axis=1))
        ah, al = a_hi[k], a_lo[k]
        part = dot(yh, ah) + dot(yl, ah) + dot(yh, al)
        if first:
            l_acc[...] = part
        else:
            l_acc[...] += part

    def left_some(start, stop):
        @pl.loop(start, stop)
        def _(k):
            left_term(k, False)

    left_term(0, True)
    r_service(1)
    left_some(1, 8)
    l_out[...] = jnp.transpose(l_acc[...])
    for j, off in enumerate(ROW_OFFSETS):
        there = pl.multiple_of(row_at(off) * 16, 16)
        remote(l_out.at[pl.ds(there, 16), :], l_in.at[j], send_sem.at[4], l_sem, row_dev(off)).start()

    r_service(2)
    raw_wait(3, 0)
    raw_wait(3, 1)
    total = r_acc[r_rows(0), :] + raw_in[0, 3] + raw_in[1, 3]
    for half in (0, 1):
        relay_wait(0, 3, half)
        relay_wait(1, 2, half)
    fin_r[...] = total + relay_in[0, 3] + relay_in[1, 2]
    remote(fin_r.at[pl.ds(other, 16), :], half_in, send_sem.at[5], half_sem, y_dev).start()

    remote(l_in, l_in, send_sem.at[4], l_sem, y_dev).wait_recv()
    left = l_out[pl.ds(pl.multiple_of(row * 16, 16), 16), :]
    for j in range(len(ROW_OFFSETS)):
        left = left + l_in[j]
    fin_l[...] = left
    out_l = pltpu.make_async_copy(fin_l, left_hbm, loc_sem.at[3])
    out_l.start()
    remote(half_in, half_in, send_sem.at[5], half_sem, y_dev).wait_recv()
    right = fin_r[pl.ds(mine, 16), :] + half_in[...]
    half_in[...] = right
    out_r = pltpu.make_async_copy(half_in, right_hbm, loc_sem.at[4])
    out_r.start()

    squares = jnp.concatenate(
        [jnp.sum(right * right, axis=0, keepdims=True), jnp.sum(left * left, axis=0, keepdims=True)], axis=0
    )
    plane_buf[0] = squares
    for j, off in enumerate(PLANE_OFFSETS):
        remote(plane_buf.at[0], plane_buf.at[j + 1], send_sem.at[6], p_sem, plane_dev(off)).start()
    n = len(PLANE_OFFSETS)
    remote(plane_buf.at[pl.ds(1, n)], plane_buf.at[pl.ds(1, n)], send_sem.at[6], p_sem, y_dev).wait_recv()
    z_buf[0] = jnp.sum(plane_buf[...], axis=0)
    for j, dz in enumerate(Z_OFFSETS):
        remote(z_buf.at[0], z_buf.at[j + 1], send_sem.at[7], z_sem, z_dev(dz)).start()

    def sent(index, rows):
        remote(a_buf.at[0, pl.ds(0, rows), :], a_buf.at[0, pl.ds(0, rows), :], send_sem.at[index], x_sem, y_dev).wait_send()

    sent(0, 240)
    sent(1, 31 * 16)
    sent(2, 14 * 16)
    sent(3, 8 * 32)
    sent(4, 240)
    sent(5, 16)
    remote(plane_buf.at[pl.ds(1, n)], plane_buf.at[pl.ds(1, n)], send_sem.at[6], p_sem, y_dev).wait_send()
    out_l.wait()
    out_r.wait()
    m = len(Z_OFFSETS)
    last = remote(z_buf.at[pl.ds(1, m)], z_buf.at[pl.ds(1, m)], send_sem.at[7], z_sem, y_dev)
    last.wait_send()
    last.wait_recv()
    mean_ref[...] = jnp.sqrt(jnp.sum(z_buf[...], axis=0) / N + EPSILON)


def body(coefficients, lambdas, right_vecs, left_vecs):
    any_spec = pl.BlockSpec(memory_space=pl.ANY)
    vmem = pltpu.VMEM
    dma = pltpu.SemaphoreType.DMA
    return pl.pallas_call(
        kernel,
        out_shape=(
            jax.ShapeDtypeStruct((16, TRIP), F32),
            jax.ShapeDtypeStruct((16, TRIP), F32),
            jax.ShapeDtypeStruct((2, TRIP), F32),
        ),
        in_specs=[any_spec] * 4,
        out_specs=(any_spec, any_spec, pl.BlockSpec(memory_space=pltpu.VMEM)),
        scratch_shapes=[
            vmem((K, 512, 256), F32),
            vmem((K, 512, 256), BF16),
            vmem((K, 512, 256), BF16),
            vmem((1, TRIP), F32),
            vmem((K, 1, TRIP), F32),
            vmem((K, TRIP, 128), F32),
            vmem((256, TRIP), F32),
            vmem((NZ, 32, TRIP), F32),
            vmem((TRIP, 512), F32),
            vmem((512, TRIP), F32),
            vmem((TRIP, 256), F32),
            vmem((256, TRIP), F32),
            vmem((2, 4, 32, TRIP), F32),
            vmem((2, 3, 32, TRIP), F32),
            vmem((2, 4, 32, TRIP), F32),
            vmem((16, TRIP), F32),
            vmem((15, 16, TRIP), F32),
            vmem((32, TRIP), F32),
            vmem((16, TRIP), F32),
            vmem((32, 2, TRIP), F32),
            vmem((16, 2, TRIP), F32),
            dma((16,)),
            dma((5,)),
            dma((8,)),
            dma,
            dma,
            dma((2, 2, 4)),
            dma((2, 2, 4)),
            dma((2, 4, 2)),
            dma((2, 4)),
            dma,
            dma,
            dma,
            dma,
        ],
        compiler_params=pltpu.CompilerParams(
            collective_id=0, has_side_effects=True, vmem_limit_bytes=56 * 1024 * 1024
        ),
    )(coefficients, lambdas.reshape(1, TRIP), right_vecs, left_vecs)


def solution(mesh):
    return jax.shard_map(
        body,
        mesh=mesh,
        in_specs=(P(None, "row", "col"), P(), P(("col", "row"), None), P(("row", "col"), None)),
        out_specs=(P(("row", "col"), None), P(("col", "row"), None), P()),
        check_vma=False,
    )
```

time: 925 us -> 66.7 us (0.07)
  waiting for transfers between devices: 663 us -> 0 us
  blocking collectives: 220 us -> 0 us
  Pallas kernels: 0 us -> 61.9 us
  matrix products: 18.7 us -> 0 us
  between operations: 14.2 us -> 0.64 us
    unnamed x4 -> x0, waiting for transfers between devices: 663 us -> none
    psum x1 -> x0, blocking collectives: 113 us -> none  [body(): lax.psum((jnp.sum(right_resid * right_resid, axis=0), jnp.sum(left_resid...]
    all_gather x2 -> x0, blocking collectives: 107 us -> none  [the longest x1 72.7 us: body(): left_rows = lax.all_gather(left_vecs, 'col', axis=0, tiled=True)]
    pallas_call x0 -> x1, Pallas kernels: none -> 61.9 us  [body(): pl.pallas_call(kernel, out_shape=(jax.ShapeDtypeStruct((16, TRIP), F32),...]
    dot_general x16 -> x0, matrix products: 18.7 us -> none  [the longest x7 8.36 us: right_term(): jnp.dot(matrices[term], weighted[term], precision=lax.Precision.HIGHEST,...]
  transfers between devices with their start and end apart: 2 -> 0, of which waited for: 2 -> 0; matrix products, arithmetic and copies ran while one was open for 1% -> 0% of each run, Pallas kernels for 0% -> 0%
where the time goes in v1:
time: 66.7 us; the launch traced here: 66.4 us
  Pallas kernels  61.9 us (93%)
  local copies, waits for them, and re-layouts  3.89 us (6%)
    pallas_call x1, Pallas kernels, body(): pl.pallas_call(kernel, out_shape=(jax.ShapeDtypeStruct((16, TRIP), F32),...  61.9 us
    unnamed x3, local copies, waits for them, and re-layouts  3.89 us

profile of v1, /device:TPU:1, one launch (start us, length us, event | category | flops | bytes accessed | tf_op | source)
XLA Modules:
  0.0 66.4 jit_solution(3711778139752955889)
XLA Ops:
  0.6 61.9 %shard_map.67 = (f32[16,256]{1,0:T(8,128)}, f32[16,256]{1,0:T(8,128)}, f32[2,256]{1,0:T(2,128)}) custom-call(f32[8,512,256]{2,1,0:T(8,128)} %a_hbm.1, f32[1,256]{1,0:T(1,128)} %bitcast.1, f32[16,256]{1,0:T(8,128)} %x_hbm.1, f32[16,256]{1,0:T(8,128)} %y_hbm.1), custom_call_target="tpu_custom_call" | custom-call | tf_op jit(solution)/shard_map/pallas_call | solution.py:322
  62.5 1.3 %copy.10 = f32[16,256]{1,0:T(8,128)} copy(f32[16,256]{1,0:T(8,128)} %get-tuple-element.6) | data formatting | bytes 32768
  63.8 1.3 %copy.11 = f32[16,256]{1,0:T(8,128)} copy(f32[16,256]{1,0:T(8,128)} %get-tuple-element.7) | data formatting | bytes 32768
  65.1 1.2 %copy.12 = f32[2,256]{1,0:T(2,128)} copy(f32[2,256]{1,0:T(2,128)} %get-tuple-element.8) | data formatting | bytes 4096

commit v2 on v1

v2 whole, which is shorter than its diff:
```python
import functools

import jax
import jax.numpy as jnp
from jax import lax
from jax.experimental import pallas as pl
from jax.experimental.pallas import tpu as pltpu
from jax.sharding import PartitionSpec as P

MESH = pl.DeviceIdType.MESH
N = 8192
K = 8
TRIP = 256
NX, NY, NZ = 4, 4, 16
EPSILON = 1e-06
F32 = jnp.float32
BF16 = jnp.bfloat16

ROW_OFFSETS = [(dx, dy, dc) for dx in (2, 1, 3, 0) for dy in (1, 0) for dc in (0, 1) if dx or dy or dc]
PLANE_OFFSETS = [(dx, dy, dc) for dx in (2, 1, 3, 0) for dy in (2, 1, 3, 0) for dc in (0, 1) if dx or dy or dc]
Z_OFFSETS = [8, 7, 9, 6, 10, 5, 11, 4, 12, 3, 13, 2, 14, 1, 15]


def split(value):
    high = value.astype(BF16)
    low = (value - high.astype(F32)).astype(BF16)
    return high, low


def dot(a, b):
    return jnp.dot(a, b, preferred_element_type=F32)


def slot(rel):
    return (rel + 4) % 16


def kernel(
    a_hbm, lam_hbm, x_hbm, y_hbm, right_ref, left_ref, mean_ref,
    a_buf, a_split, lam_buf, w_row, w_col, x_buf, y_buf, y_t, r_acc, l_acc, l_out,
    relay_in, relay_out, raw_in, last_in, base, half_in, l_in, plane_buf, z_buf,
    a_sem, loc_sem, send_sem, x_sem, y_sem, yr_sem, yd_sem, rr_sem, raw_sem, half_sem, l_sem, p_sem, z_sem,
):
    row, col = lax.axis_index("row"), lax.axis_index("col")
    y_lo, x, core = row // 8, (row // 2) % 4, row % 2
    z, y_hi = col // 2, col % 2

    def row_at(off):
        dx, dy, dc = off
        return ((y_lo + dy) % 2) * 8 + ((x + dx) % 4) * 2 + (core + dc) % 2

    def row_dev(off):
        return (row_at(off), col)

    def plane_dev(off):
        dx, dy, dc = off
        yy = (y_hi * 2 + y_lo + dy) % 4
        return ((yy % 2) * 8 + ((x + dx) % 4) * 2 + (core + dc) % 2, z * 2 + yy // 2)

    def z_dev(dz):
        return (row, ((z + dz + 16) % 16) * 2 + y_hi)

    y_dev = (row, z * 2 + (1 - y_hi))

    def remote(src, dst, ssem, rsem, dev):
        return pltpu.make_async_remote_copy(
            src_ref=src, dst_ref=dst, send_sem=ssem, recv_sem=rsem, device_id=dev, device_id_type=MESH
        )

    def other_dev(dz):
        return (row, ((z + dz + 16) % 16) * 2 + (1 - y_hi))

    barrier = pltpu.get_barrier_semaphore()
    partners = [row_dev(off) for off in ROW_OFFSETS] + [z_dev(1), z_dev(-1), z_dev(2), z_dev(-2)]
    partners += [y_dev, other_dev(1), other_dev(-1)]
    for dev in partners:
        pl.semaphore_signal(barrier, inc=1, device_id=dev, device_id_type=MESH)

    my_x = pl.multiple_of(row * 16, 16)
    mine, other = pl.multiple_of(y_hi * 16, 16), pl.multiple_of((1 - y_hi) * 16, 16)
    local = [
        pltpu.make_async_copy(lam_hbm, lam_buf, loc_sem.at[0]),
        pltpu.make_async_copy(x_hbm, x_buf.at[pl.ds(my_x, 16), :], loc_sem.at[1]),
        pltpu.make_async_copy(y_hbm, y_buf.at[slot(0), pl.ds(mine, 16), :], loc_sem.at[2]),
    ]
    for copy in local:
        copy.start()
    for j in range(NZ):
        rows = pl.multiple_of(((z + j - 4 + 16) % 16) * 32, 32)
        pltpu.make_async_copy(
            a_hbm.at[:, pl.ds(rows, 32), :], a_buf.at[:, pl.ds(j * 32, 32), :], a_sem.at[j]
        ).start()
    pl.semaphore_wait(barrier, len(partners))

    def y_slot(rel, chunk=0):
        return y_buf.at[slot(rel), pl.ds(mine if chunk == 0 else other, 16), :]

    def y_send(rel, to, sem, dev):
        src = y_hbm if rel == 0 else y_slot(rel)
        remote(src, y_slot(to), send_sem.at[1], sem, dev).start()

    def y_wait(rel, chunk, sem):
        ref = y_slot(rel, chunk)
        remote(ref, ref, send_sem.at[1], sem, y_dev).wait_recv()

    def y_relays(step):
        for d, sign in ((0, 1), (1, -1)):
            rel = -2 * step * sign
            if sign > 0 or step < 3:
                y_send(rel, rel - 2 * sign, yr_sem.at[0, d, step], z_dev(2 * sign))
            if sign > 0 and step == 3:
                y_send(rel, rel - 2 * sign, yr_sem.at[1, 0, 0], other_dev(2 * sign))

    def y_drops(step):
        for d, sign in ((0, 1), (1, -1)):
            rel = -2 * step * sign
            y_send(rel, rel - sign, yd_sem.at[0, d, step], z_dev(sign))

    def y_copies(step):
        for d, sign in ((0, 1), (1, -1)):
            rel = -2 * step * sign
            if step > 0:
                y_send(rel, rel, yr_sem.at[1, d, step], y_dev)
            elif sign > 0:
                y_send(rel, rel, y_sem, y_dev)
        for d, sign in ((0, 1), (1, -1)):
            rel = -2 * step * sign
            y_send(rel, rel - sign, yd_sem.at[1, d, step], other_dev(sign))

    def y_service(step):
        if step == 3:
            y_wait_copy(1)
        for d, sign in ((0, 1), (1, -1)):
            y_wait(-2 * step * sign, 0, yr_sem.at[0, d, step - 1])
        y_relays(step)
        y_drops(step)
        if step > 1:
            y_copies(step)

    def y_wait_copy(step):
        for d, sign in ((0, 1), (1, -1)):
            y_wait(-2 * step * sign, 1, yr_sem.at[1, d, step])

    def y_wait_drop(step):
        for chunk in (0, 1):
            for d, sign in ((0, -1), (1, 1)):
                y_wait(sign * (2 * step + 1), chunk, yd_sem.at[chunk, d, step])

    y_relays(0)
    for off in ROW_OFFSETS:
        remote(x_hbm, x_buf.at[pl.ds(my_x, 16), :], send_sem.at[0], x_sem, row_dev(off)).start()
    y_drops(0)

    local[0].wait()
    lam = lam_buf[...]
    terms = [jnp.ones_like(lam), lam]
    while len(terms) < K:
        terms.append(2.0 * lam * terms[-1] - terms[-2])
    for k in range(K):
        w_row[k] = terms[k]
    lam_col = jnp.transpose(jnp.broadcast_to(lam, (128, TRIP)))
    w_col[0] = jnp.ones_like(lam_col)
    w_col[1] = lam_col
    for k in range(2, K):
        w_col[k] = 2.0 * lam_col * w_col[k - 1] - w_col[k - 2]

    @pl.loop(0, NZ)
    def _(j):
        rows = pl.ds(pl.multiple_of(j * 32, 32), 32)
        pltpu.make_async_copy(a_hbm.at[:, pl.ds(0, 32), :], a_buf.at[:, rows, :], a_sem.at[j]).wait()
        part, start = j // 8, pl.multiple_of((j % 8) * 32, 32)
        for k in range(K):
            high, low = split(a_buf[k, rows, :])
            a_split[k, part, pl.ds(start, 32), :] = high
            a_split[k, part, pl.ds(start + 256, 32), :] = low

    y_service(1)
    local[1].wait()
    remote(x_buf.at[pl.ds(0, 240), :], x_buf.at[pl.ds(0, 240), :], send_sem.at[0], x_sem, y_dev).wait_recv()

    def right_half(part):
        rows = pl.ds(part * 256, 256)

        def term(k):
            xh, xl = split(x_buf[...] * w_row[k])
            both = dot(a_split[k, part], xh)
            return both[:256] + both[256:] + dot(a_split[k, part, :256, :], xl)

        r_acc[rows, :] = term(0)
        for k in range(1, K):
            r_acc[rows, :] += term(k)

    def half_rows(half):
        return pl.ds(mine if half == 0 else other, 16)

    def r_block(rel, half):
        return pl.ds(slot(rel) * 32 + (mine if half == 0 else other), 16)

    def relay(rel, half, up, src):
        i, d = ((8 - rel) // 2 if up else (rel + 6) // 2), (0 if up else 1)
        last = abs(rel) == 2
        dst = last_in.at[d, half] if last else relay_in.at[d, i, half_rows(half), :]
        dz = 2 if up else -2
        return remote(src, dst, send_sem.at[2], rr_sem.at[d, i, half], other_dev(dz) if last and half == 1 else z_dev(dz))

    def raw(rel):
        up = rel > 0
        i, d = ((7 - rel) // 2 if up else (rel + 7) // 2), (0 if up else 1)
        rows = pl.ds(slot(rel) * 32, 32)
        return remote(r_acc.at[rows, :], raw_in.at[d, i], send_sem.at[3], raw_sem.at[d, i], z_dev(1 if up else -1))

    def raw_wait(i, d):
        remote(raw_in.at[d, i], raw_in.at[d, i], send_sem.at[3], raw_sem.at[d, i], y_dev).wait_recv()

    def r_service(step):
        for d, up in ((1, False), (0, True)):
            raw_wait(step, d)
        for half in (1, 0):
            for d, up in ((1, False), (0, True)):
                rel = 6 - 2 * step if up else 2 * step - 6
                hs = half_rows(half)
                total = r_acc[r_block(rel, half), :] + raw_in[d, step, hs, :]
                if up or step > 0:
                    i = step if up else step - 1
                    ref = relay_in.at[d, i, hs, :]
                    remote(ref, ref, send_sem.at[2], rr_sem.at[d, i, half], y_dev).wait_recv()
                    total = total + relay_in[d, i, hs, :]
                relay_out[d, step, hs, :] = total
                relay(rel, half, up, relay_out.at[d, step, hs, :]).start()

    right_half(1)
    for half in (1, 0):
        relay(8, half, True, r_acc.at[r_block(8, half), :]).start()
    for rel in (-7, 7):
        raw(rel).start()
    y_copies(0)
    y_copies(1)
    right_half(0)

    y_service(2)
    r_service(0)
    for rel in (-5, 5):
        raw(rel).start()
    y_service(3)

    def turn(part):
        for i in (0, 1):
            y_t[part, :, i * 128 : (i + 1) * 128] = jnp.transpose(
                jnp.concatenate([y_buf[8 * part + 4 * i + j] for j in range(4)], axis=0)
            )

    def left_half(part):
        def term(k):
            w = w_col[k]
            yh, yl = split(y_t[part] * jnp.concatenate([w, w], axis=1))
            both = dot(jnp.concatenate([yh, yl], axis=0), a_split[k, part, :256, :])
            return both[:256] + both[256:] + dot(yh, a_split[k, part, 256:, :])

        for k in range(K):
            if part == 0 and k == 0:
                l_acc[...] = term(k)
            else:
                l_acc[...] += term(k)

    local[2].wait()
    y_wait(0, 1, y_sem)
    y_wait_copy(2)
    y_wait_drop(0)
    y_wait_drop(1)
    turn(0)
    left_half(0)
    r_service(1)
    for rel in (-3, 3, -1, 1):
        raw(rel).start()
    y_wait(-8, 0, yr_sem.at[0, 0, 3])
    y_wait(-8, 1, yr_sem.at[1, 0, 0])
    y_wait_copy(3)
    y_wait_drop(2)
    y_wait_drop(3)
    turn(1)
    left_half(1)
    l_out[...] = jnp.transpose(l_acc[...])
    for j, off in enumerate(ROW_OFFSETS):
        there = pl.multiple_of(row_at(off) * 16, 16)
        remote(l_out.at[pl.ds(there, 16), :], l_in.at[j], send_sem.at[4], l_sem, row_dev(off)).start()
    raw_wait(3, 0)
    raw_wait(3, 1)
    base[...] = r_acc[pl.ds(slot(0) * 32, 32), :] + raw_in[0, 3] + raw_in[1, 3]
    remote(base.at[pl.ds(other, 16), :], half_in, send_sem.at[5], half_sem, y_dev).start()
    r_service(2)

    remote(l_in, l_in, send_sem.at[4], l_sem, y_dev).wait_recv()
    left = l_out[pl.ds(pl.multiple_of(row * 16, 16), 16), :]
    for j in range(len(ROW_OFFSETS)):
        left = left + l_in[j]
    left_ref[...] = left
    remote(half_in, half_in, send_sem.at[5], half_sem, y_dev).wait_recv()
    right = base[pl.ds(mine, 16), :] + half_in[...]
    for d, i in ((0, 3), (1, 2)):
        for half in (0, 1):
            ref = last_in.at[d, half]
            remote(ref, ref, send_sem.at[2], rr_sem.at[d, i, half], y_dev).wait_recv()
            right = right + last_in[d, half]
    right_ref[...] = right

    squares = jnp.concatenate(
        [jnp.sum(right * right, axis=0, keepdims=True), jnp.sum(left * left, axis=0, keepdims=True)], axis=0
    )
    plane_buf[0] = squares
    for j, off in enumerate(PLANE_OFFSETS):
        remote(plane_buf.at[0], plane_buf.at[j + 1], send_sem.at[6], p_sem, plane_dev(off)).start()
    n = len(PLANE_OFFSETS)
    remote(plane_buf.at[pl.ds(1, n)], plane_buf.at[pl.ds(1, n)], send_sem.at[6], p_sem, y_dev).wait_recv()
    z_buf[0] = jnp.sum(plane_buf[...], axis=0)
    for j, dz in enumerate(Z_OFFSETS):
        remote(z_buf.at[0], z_buf.at[j + 1], send_sem.at[7], z_sem, z_dev(dz)).start()

    def sent(index, rows):
        remote(a_buf.at[0, pl.ds(0, rows), :], a_buf.at[0, pl.ds(0, rows), :], send_sem.at[index], x_sem, y_dev).wait_send()

    sent(0, 240)
    sent(1, 31 * 16)
    sent(2, 14 * 16)
    sent(3, 8 * 32)
    sent(4, 240)
    sent(5, 16)
    remote(plane_buf.at[pl.ds(1, n)], plane_buf.at[pl.ds(1, n)], send_sem.at[6], p_sem, y_dev).wait_send()
    m = len(Z_OFFSETS)
    last = remote(z_buf.at[pl.ds(1, m)], z_buf.at[pl.ds(1, m)], send_sem.at[7], z_sem, y_dev)
    last.wait_send()
    last.wait_recv()
    mean_ref[...] = jnp.sqrt(jnp.sum(z_buf[...], axis=0) / N + EPSILON)


def finish(right_ref, left_ref, mean_ref, right_out, left_out, mean_out, sem):
    copies = [
        pltpu.make_async_copy(right_ref, right_out, sem.at[0]),
        pltpu.make_async_copy(left_ref, left_out, sem.at[1]),
        pltpu.make_async_copy(mean_ref, mean_out, sem.at[2]),
    ]
    for copy in copies:
        copy.start()
    for copy in copies:
        copy.wait()


def body(coefficients, lambdas, right_vecs, left_vecs):
    any_spec = pl.BlockSpec(memory_space=pl.ANY)
    vmem = pltpu.VMEM
    dma = pltpu.SemaphoreType.DMA
    shapes = ((16, TRIP), (16, TRIP), (2, TRIP))
    vmem_spec = pl.BlockSpec(memory_space=vmem)
    results = pl.pallas_call(
        kernel,
        out_shape=tuple(vmem(shape, F32) for shape in shapes),
        in_specs=[any_spec] * 4,
        out_specs=(vmem_spec,) * 3,
        scratch_shapes=[
            vmem((K, 512, 256), F32),
            vmem((K, 2, 512, 256), BF16),
            vmem((1, TRIP), F32),
            vmem((K, 1, TRIP), F32),
            vmem((K, TRIP, 128), F32),
            vmem((256, TRIP), F32),
            vmem((NZ, 32, TRIP), F32),
            vmem((2, TRIP, 256), F32),
            vmem((512, TRIP), F32),
            vmem((TRIP, 256), F32),
            vmem((256, TRIP), F32),
            vmem((2, 3, 32, TRIP), F32),
            vmem((2, 3, 32, TRIP), F32),
            vmem((2, 4, 32, TRIP), F32),
            vmem((2, 2, 16, TRIP), F32),
            vmem((32, TRIP), F32),
            vmem((16, TRIP), F32),
            vmem((15, 16, TRIP), F32),
            vmem((32, 2, TRIP), F32),
            vmem((16, 2, TRIP), F32),
            dma((16,)),
            dma((3,)),
            dma((8,)),
            dma,
            dma,
            dma((2, 2, 4)),
            dma((2, 2, 4)),
            dma((2, 4, 2)),
            dma((2, 4)),
            dma,
            dma,
            dma,
            dma,
        ],
        compiler_params=pltpu.CompilerParams(
            collective_id=0, has_side_effects=True, vmem_limit_bytes=56 * 1024 * 1024
        ),
    )(coefficients, lambdas.reshape(1, TRIP), right_vecs, left_vecs)
    return pl.pallas_call(
        finish,
        out_shape=tuple(jax.ShapeDtypeStruct(shape, F32) for shape in shapes),
        in_specs=[vmem_spec] * 3,
        out_specs=(any_spec,) * 3,
        scratch_shapes=[dma((3,))],
    )(*[pltpu.with_memory_space_constraint(result, vmem) for result in results])


def solution(mesh):
    return jax.shard_map(
        body,
        mesh=mesh,
        in_specs=(P(None, "row", "col"), P(), P(("col", "row"), None), P(("row", "col"), None)),
        out_specs=(P(("row", "col"), None), P(("col", "row"), None), P()),
        check_vma=False,
    )
```

time: 66.7 us -> 54.8 us (0.82)
  Pallas kernels: 61.9 us -> 54.1 us
  local copies, waits for them, and re-layouts: 3.89 us -> 0 us
    pallas_call x1 -> x2, Pallas kernels: 61.9 us -> 54.1 us  [the longest x1 53.4 us: body(): pl.pallas_call(kernel, out_shape=tuple((vmem(shape, F32) for shape in sha...]
    unnamed x3 -> x0, local copies, waits for them, and re-layouts: 3.89 us -> none
where the time goes in v2:
time: 54.8 us; the launch traced here: 54.7 us
  Pallas kernels  54.1 us (99%)
  between operations  0.64 us (1%)
    pallas_call x1, Pallas kernels, body(): pl.pallas_call(kernel, out_shape=tuple((vmem(shape, F32) for shape in sha...  53.4 us

profile of v2, /device:TPU:1, one launch (start us, length us, event | category | flops | bytes accessed | tf_op | source)
XLA Modules:
  0.0 54.7 jit_solution(13915146833593748266)
XLA Ops:
  0.6 53.4 %shard_map.67 = (f32[16,256]{1,0:T(8,128)S(1)}, f32[16,256]{1,0:T(8,128)S(1)}, f32[2,256]{1,0:T(2,128)S(1)}) custom-call(f32[8,512,256]{2,1,0:T(8,128)} %a_hbm.1, f32[1,256]{1,0:T(1,128)} %bitcast.1, f32[16,256]{1,0:T(8,128)} %x_hbm.1, f32[16,256]{1,0:T(8,128)} %y_hbm.1), custom_call_target="tpu_custom_call" | custom-call | tf_op jit(solution)/shard_map/pallas_call | solution.py:353
  54.1 0.6 %shard_map.68 = (f32[16,256]{1,0:T(8,128)}, f32[16,256]{1,0:T(8,128)}, f32[2,256]{1,0:T(2,128)}) custom-call(f32[16,256]{1,0:T(8,128)S(1)} %get-tuple-element.6.right_ref, f32[16,256]{1,0:T(8,128)S(1)} %get-tuple-element.7.left_ref, f32[2,256]{1,0:T(2,128)S(1)} %get-tuple-element.8.mean_ref), custom_call_target="tpu_custom_call" | custom-call | tf_op jit(solution)/shard_map/pallas_call | solution.py:397

commit v3 on v2

--- a/solution.py
+++ b/solution.py
@@ -17,6 +17,8 @@
 BF16 = jnp.bfloat16
 
 ROW_OFFSETS = [(dx, dy, dc) for dx in (2, 1, 3, 0) for dy in (1, 0) for dc in (0, 1) if dx or dy or dc]
+NEAR = [4, -4, 3, -3, 2, -2, 1, -1]
+FAR = [(8, 4), (7, 3), (-7, -3), (6, 2), (-6, -2), (5, 1), (-5, -1)]
 PLANE_OFFSETS = [(dx, dy, dc) for dx in (2, 1, 3, 0) for dy in (2, 1, 3, 0) for dc in (0, 1) if dx or dy or dc]
 Z_OFFSETS = [8, 7, 9, 6, 10, 5, 11, 4, 12, 3, 13, 2, 14, 1, 15]
 
@@ -38,8 +40,8 @@
 def kernel(
     a_hbm, lam_hbm, x_hbm, y_hbm, right_ref, left_ref, mean_ref,
     a_buf, a_split, lam_buf, w_row, w_col, x_buf, y_buf, y_t, r_acc, l_acc, l_out,
-    relay_in, relay_out, raw_in, last_in, base, half_in, l_in, plane_buf, z_buf,
-    a_sem, loc_sem, send_sem, x_sem, y_sem, yr_sem, yd_sem, rr_sem, raw_sem, half_sem, l_sem, p_sem, z_sem,
+    mid_in, mid_out, fin_in, fin_out, cross_in, l_in, plane_buf, z_buf,
+    a_sem, loc_sem, send_sem, x_sem, y_sem, mid_sem, fin_sem, cross_sem, l_sem, p_sem, z_sem,
 ):
     row, col = lax.axis_index("row"), lax.axis_index("col")
     y_lo, x, core = row // 8, (row // 2) % 4, row % 2
@@ -71,8 +73,7 @@
         return (row, ((z + dz + 16) % 16) * 2 + (1 - y_hi))
 
     barrier = pltpu.get_barrier_semaphore()
-    partners = [row_dev(off) for off in ROW_OFFSETS] + [z_dev(1), z_dev(-1), z_dev(2), z_dev(-2)]
-    partners += [y_dev, other_dev(1), other_dev(-1)]
+    partners = [row_dev(off) for off in ROW_OFFSETS] + [z_dev(dz) for dz in NEAR] + [y_dev]
     for dev in partners:
         pl.semaphore_signal(barrier, inc=1, device_id=dev, device_id_type=MESH)
 
@@ -95,61 +96,21 @@
     def y_slot(rel, chunk=0):
         return y_buf.at[slot(rel), pl.ds(mine if chunk == 0 else other, 16), :]
 
-    def y_send(rel, to, sem, dev):
+    def y_send(rel, to, chunk, dev):
         src = y_hbm if rel == 0 else y_slot(rel)
-        remote(src, y_slot(to), send_sem.at[1], sem, dev).start()
-
-    def y_wait(rel, chunk, sem):
+        remote(src, y_slot(to), send_sem.at[1], y_sem.at[chunk, slot(to)], dev).start()
+
+    def y_wait(rel, chunk):
         ref = y_slot(rel, chunk)
-        remote(ref, ref, send_sem.at[1], sem, y_dev).wait_recv()
-
-    def y_relays(step):
-        for d, sign in ((0, 1), (1, -1)):
-            rel = -2 * step * sign
-            if sign > 0 or step < 3:
-                y_send(rel, rel - 2 * sign, yr_sem.at[0, d, step], z_dev(2 * sign))
-            if sign > 0 and step == 3:
-                y_send(rel, rel - 2 * sign, yr_sem.at[1, 0, 0], other_dev(2 * sign))
-
-    def y_drops(step):
-        for d, sign in ((0, 1), (1, -1)):
-            rel = -2 * step * sign
-            y_send(rel, rel - sign, yd_sem.at[0, d, step], z_dev(sign))
-
-    def y_copies(step):
-        for d, sign in ((0, 1), (1, -1)):
-            rel = -2 * step * sign
-            if step > 0:
-                y_send(rel, rel, yr_sem.at[1, d, step], y_dev)
-            elif sign > 0:
-                y_send(rel, rel, y_sem, y_dev)
-        for d, sign in ((0, 1), (1, -1)):
-            rel = -2 * step * sign
-            y_send(rel, rel - sign, yd_sem.at[1, d, step], other_dev(sign))
-
-    def y_service(step):
-        if step == 3:
-            y_wait_copy(1)
-        for d, sign in ((0, 1), (1, -1)):
-            y_wait(-2 * step * sign, 0, yr_sem.at[0, d, step - 1])
-        y_relays(step)
-        y_drops(step)
-        if step > 1:
-            y_copies(step)
-
-    def y_wait_copy(step):
-        for d, sign in ((0, 1), (1, -1)):
-            y_wait(-2 * step * sign, 1, yr_sem.at[1, d, step])
-
-    def y_wait_drop(step):
-        for chunk in (0, 1):
-            for d, sign in ((0, -1), (1, 1)):
-                y_wait(sign * (2 * step + 1), chunk, yd_sem.at[chunk, d, step])
-
-    y_relays(0)
+        remote(ref, ref, send_sem.at[1], y_sem.at[chunk, slot(rel)], y_dev).wait_recv()
+
+    for dz in NEAR[:2]:
+        y_send(0, -dz, 0, z_dev(dz))
     for off in ROW_OFFSETS:
         remote(x_hbm, x_buf.at[pl.ds(my_x, 16), :], send_sem.at[0], x_sem, row_dev(off)).start()
-    y_drops(0)
+    for dz in NEAR[2:]:
+        y_send(0, -dz, 0, z_dev(dz))
+    y_send(0, 0, 1, y_dev)
 
     local[0].wait()
     lam = lam_buf[...]
@@ -174,7 +135,20 @@
             a_split[k, part, pl.ds(start, 32), :] = high
             a_split[k, part, pl.ds(start + 256, 32), :] = low
 
-    y_service(1)
+    def y_far(chunk):
+        for far, dz in FAR:
+            y_send(-4 if dz > 0 else 4, -far, chunk, z_dev(dz) if chunk == 0 else other_dev(dz))
+
+    def y_near():
+        for dz in NEAR[2:]:
+            y_wait(dz, 0)
+        for dz in NEAR:
+            y_send(dz, dz, 1, y_dev)
+
+    y_wait(4, 0)
+    y_wait(-4, 0)
+    y_far(0)
+    y_near()
     local[1].wait()
     remote(x_buf.at[pl.ds(0, 240), :], x_buf.at[pl.ds(0, 240), :], send_sem.at[0], x_sem, y_dev).wait_recv()
 
@@ -190,58 +164,46 @@
         for k in range(1, K):
             r_acc[rows, :] += term(k)
 
-    def half_rows(half):
-        return pl.ds(mine if half == 0 else other, 16)
-
-    def r_block(rel, half):
-        return pl.ds(slot(rel) * 32 + (mine if half == 0 else other), 16)
-
-    def relay(rel, half, up, src):
-        i, d = ((8 - rel) // 2 if up else (rel + 6) // 2), (0 if up else 1)
-        last = abs(rel) == 2
-        dst = last_in.at[d, half] if last else relay_in.at[d, i, half_rows(half), :]
-        dz = 2 if up else -2
-        return remote(src, dst, send_sem.at[2], rr_sem.at[d, i, half], other_dev(dz) if last and half == 1 else z_dev(dz))
-
-    def raw(rel):
-        up = rel > 0
-        i, d = ((7 - rel) // 2 if up else (rel + 7) // 2), (0 if up else 1)
-        rows = pl.ds(slot(rel) * 32, 32)
-        return remote(r_acc.at[rows, :], raw_in.at[d, i], send_sem.at[3], raw_sem.at[d, i], z_dev(1 if up else -1))
-
-    def raw_wait(i, d):
-        remote(raw_in.at[d, i], raw_in.at[d, i], send_sem.at[3], raw_sem.at[d, i], y_dev).wait_recv()
-
-    def r_service(step):
-        for d, up in ((1, False), (0, True)):
-            raw_wait(step, d)
-        for half in (1, 0):
-            for d, up in ((1, False), (0, True)):
-                rel = 6 - 2 * step if up else 2 * step - 6
-                hs = half_rows(half)
-                total = r_acc[r_block(rel, half), :] + raw_in[d, step, hs, :]
-                if up or step > 0:
-                    i = step if up else step - 1
-                    ref = relay_in.at[d, i, hs, :]
-                    remote(ref, ref, send_sem.at[2], rr_sem.at[d, i, half], y_dev).wait_recv()
-                    total = total + relay_in[d, i, hs, :]
-                relay_out[d, step, hs, :] = total
-                relay(rel, half, up, relay_out.at[d, step, hs, :]).start()
+    def cross(rel):
+        rows = pl.ds(slot(rel) * 32 + other, 16)
+        n = slot(rel)
+        return remote(r_acc.at[rows, :], cross_in.at[n], send_sem.at[5], cross_sem.at[n], y_dev)
+
+    def pair(rel):
+        ref = cross_in.at[slot(rel)]
+        remote(ref, ref, send_sem.at[5], cross_sem.at[slot(rel)], y_dev).wait_recv()
+        return r_acc[pl.ds(slot(rel) * 32 + mine, 16), :] + cross_in[slot(rel)]
+
+    def r_far():
+        for i, (far, dz) in enumerate(FAR):
+            mid_out[i] = pair(far)
+            remote(mid_out.at[i], mid_in.at[i], send_sem.at[2], mid_sem.at[i], z_dev(dz)).start()
+
+    def r_send(i, value):
+        fin_out[i] = value
+        remote(fin_out.at[i], fin_in.at[i], send_sem.at[3], fin_sem.at[i], z_dev(NEAR[i])).start()
+
+    def r_relay():
+        for j, dz in enumerate(NEAR[:2]):
+            total = pair(dz)
+            for i, (_, hop) in enumerate(FAR):
+                if hop * dz > 0:
+                    remote(mid_in.at[i], mid_in.at[i], send_sem.at[2], mid_sem.at[i], y_dev).wait_recv()
+                    total = total + mid_in[i]
+            r_send(j, total)
+
+    def r_near():
+        for i, dz in enumerate(NEAR[2:]):
+            r_send(i + 2, pair(dz))
 
     right_half(1)
-    for half in (1, 0):
-        relay(8, half, True, r_acc.at[r_block(8, half), :]).start()
-    for rel in (-7, 7):
-        raw(rel).start()
-    y_copies(0)
-    y_copies(1)
+    for rel in (8, 7, -7, 6, -6, 5, -5, 4):
+        cross(rel).start()
+    y_far(1)
     right_half(0)
-
-    y_service(2)
-    r_service(0)
-    for rel in (-5, 5):
-        raw(rel).start()
-    y_service(3)
+    r_far()
+    for rel in (-4, 3, -3, 2, -2, 1, -1, 0):
+        cross(rel).start()
 
     def turn(part):
         for i in (0, 1):
@@ -263,44 +225,36 @@
                 l_acc[...] += term(k)
 
     local[2].wait()
-    y_wait(0, 1, y_sem)
-    y_wait_copy(2)
-    y_wait_drop(0)
-    y_wait_drop(1)
+    for rel in [0] + NEAR:
+        if rel != 4:
+            y_wait(rel, 1)
     turn(0)
     left_half(0)
-    r_service(1)
-    for rel in (-3, 3, -1, 1):
-        raw(rel).start()
-    y_wait(-8, 0, yr_sem.at[0, 0, 3])
-    y_wait(-8, 1, yr_sem.at[1, 0, 0])
-    y_wait_copy(3)
-    y_wait_drop(2)
-    y_wait_drop(3)
+    y_wait(4, 1)
+    for far, _ in FAR:
+        y_wait(-far, 0)
+        y_wait(-far, 1)
     turn(1)
     left_half(1)
     l_out[...] = jnp.transpose(l_acc[...])
     for j, off in enumerate(ROW_OFFSETS):
         there = pl.multiple_of(row_at(off) * 16, 16)
         remote(l_out.at[pl.ds(there, 16), :], l_in.at[j], send_sem.at[4], l_sem, row_dev(off)).start()
-    raw_wait(3, 0)
-    raw_wait(3, 1)
-    base[...] = r_acc[pl.ds(slot(0) * 32, 32), :] + raw_in[0, 3] + raw_in[1, 3]
-    remote(base.at[pl.ds(other, 16), :], half_in, send_sem.at[5], half_sem, y_dev).start()
-    r_service(2)
+    r_relay()
+    r_near()
+    right = pair(0)
 
     remote(l_in, l_in, send_sem.at[4], l_sem, y_dev).wait_recv()
     left = l_out[pl.ds(pl.multiple_of(row * 16, 16), 16), :]
     for j in range(len(ROW_OFFSETS)):
         left = left + l_in[j]
     left_ref[...] = left
-    remote(half_in, half_in, send_sem.at[5], half_sem, y_dev).wait_recv()
-    right = base[pl.ds(mine, 16), :] + half_in[...]
-    for d, i in ((0, 3), (1, 2)):
-        for half in (0, 1):
-            ref = last_in.at[d, half]
-            remote(ref, ref, send_sem.at[2], rr_sem.at[d, i, half], y_dev).wait_recv()
-            right = right + last_in[d, half]
+    for i in range(2, 8):
+        remote(fin_in.at[i], fin_in.at[i], send_sem.at[3], fin_sem.at[i], y_dev).wait_recv()
+        right = right + fin_in[i]
+    for i in (0, 1):
+        remote(fin_in.at[i], fin_in.at[i], send_sem.at[3], fin_sem.at[i], y_dev).wait_recv()
+        right = right + fin_in[i]
     right_ref[...] = right
 
     squares = jnp.concatenate(
@@ -320,10 +274,10 @@
 
     sent(0, 240)
     sent(1, 31 * 16)
-    sent(2, 14 * 16)
-    sent(3, 8 * 32)
+    sent(2, 7 * 16)
+    sent(3, 8 * 16)
     sent(4, 240)
-    sent(5, 16)
+    sent(5, 256)
     remote(plane_buf.at[pl.ds(1, n)], plane_buf.at[pl.ds(1, n)], send_sem.at[6], p_sem, y_dev).wait_send()
     m = len(Z_OFFSETS)
     last = remote(z_buf.at[pl.ds(1, m)], z_buf.at[pl.ds(1, m)], send_sem.at[7], z_sem, y_dev)
@@ -367,12 +321,11 @@
             vmem((512, TRIP), F32),
             vmem((TRIP, 256), F32),
             vmem((256, TRIP), F32),
-            vmem((2, 3, 32, TRIP), F32),
-            vmem((2, 3, 32, TRIP), F32),
-            vmem((2, 4, 32, TRIP), F32),
-            vmem((2, 2, 16, TRIP), F32),
-            vmem((32, TRIP), F32),
-            vmem((16, TRIP), F32),
+            vmem((7, 16, TRIP), F32),
+            vmem((7, 16, TRIP), F32),
+            vmem((8, 16, TRIP), F32),
+            vmem((8, 16, TRIP), F32),
+            vmem((NZ, 16, TRIP), F32),
             vmem((15, 16, TRIP), F32),
             vmem((32, 2, TRIP), F32),
             vmem((16, 2, TRIP), F32),
@@ -380,12 +333,10 @@
             dma((3,)),
             dma((8,)),
             dma,
-            dma,
-            dma((2, 2, 4)),
-            dma((2, 2, 4)),
-            dma((2, 4, 2)),
-            dma((2, 4)),
-            dma,
+            dma((2, NZ)),
+            dma((7,)),
+            dma((8,)),
+            dma((NZ,)),
             dma,
             dma,
             dma,

time: 54.8 us -> 54.4 us (level)
  no operation moved by 1% of the time
where the time goes in v3:
time: 54.4 us; the launch traced here: 54.3 us
  Pallas kernels  53.6 us (99%)
  between operations  0.64 us (1%)
    pallas_call x1, Pallas kernels, body(): pl.pallas_call(kernel, out_shape=tuple((vmem(shape, F32) for shape in sha...  53 us

profile of v3, /device:TPU:1, one launch (start us, length us, event | category | flops | bytes accessed | tf_op | source)
XLA Modules:
  0.0 54.3 jit_solution(15863504873701777485)
XLA Ops:
  0.6 53.0 %shard_map.67 = (f32[16,256]{1,0:T(8,128)S(1)}, f32[16,256]{1,0:T(8,128)S(1)}, f32[2,256]{1,0:T(2,128)S(1)}) custom-call(f32[8,512,256]{2,1,0:T(8,128)} %a_hbm.1, f32[1,256]{1,0:T(1,128)} %bitcast.1, f32[16,256]{1,0:T(8,128)} %x_hbm.1, f32[16,256]{1,0:T(8,128)} %y_hbm.1), custom_call_target="tpu_custom_call" | custom-call | tf_op jit(solution)/shard_map/pallas_call | solution.py:307
  53.6 0.6 %shard_map.68 = (f32[16,256]{1,0:T(8,128)}, f32[16,256]{1,0:T(8,128)}, f32[2,256]{1,0:T(2,128)}) custom-call(f32[16,256]{1,0:T(8,128)S(1)} %get-tuple-element.6.right_ref, f32[16,256]{1,0:T(8,128)S(1)} %get-tuple-element.7.left_ref, f32[2,256]{1,0:T(2,128)S(1)} %get-tuple-element.8.mean_ref), custom_call_target="tpu_custom_call" | custom-call | tf_op jit(solution)/shard_map/pallas_call | solution.py:348
